TPU v7x, 32 devices: a whole 2x2x4 slice. The times are simulated.
32 devices in a mesh: frame: 4 (over y, x), row: 8 (over z, core).
Axes of the slice: x: 2, y: 2, z: 4, core: 2. Of those that a mesh axis runs over, the one named last changes fastest.
Arguments:
- residual_in: bfloat16 [4, 8, 64, 768], P('frame', 'row'), may hold values from -6 to 6
- q_spatial: bfloat16 [4, 8, 64, 768], P('frame', 'row'), may hold values from -250 to 250
- k_spatial: bfloat16 [4, 8, 64, 768], P('frame', 'row'), may hold values from -250 to 250
- v_spatial: bfloat16 [4, 8, 64, 768], P('frame', 'row'), may hold values from -6 to 6
- q_temporal: bfloat16 [4, 8, 64, 768], P('frame', 'row'), may hold values from -250 to 250
- k_temporal: bfloat16 [4, 8, 64, 768], P('frame', 'row'), may hold values from -250 to 250
- conv_weight: float32 [3, 3, 768], replicated, may hold values from -2 to 2
- conv_bias: float32 [768], replicated, may hold values from -3 to 3
Outputs:
- spatial_out: bfloat16 [4, 8, 64, 768], P('frame', 'row')
- block_out: bfloat16 [4, 8, 64, 768], P('frame', 'row')
All inputs are finite; a program needn't handle non-finite values.
Results may differ from a plain program's by a relative error of at most 0.0061.
Values may be sent and summed in bfloat16 or wider, within the bound.
A program may use at most 64 MiB of HBM per device.

v0:
```python
import math
import jax
import jax.numpy as jnp
from jax import lax
from jax.sharding import PartitionSpec as P

HEADS = 12
HEAD_DIM = 64


def padded(block, sides, width):
    for axis, dim in sides:
        count = lax.axis_size(axis)
        forward = [(i, i + 1) for i in range(count - 1)]
        backward = [(target, source) for source, target in forward]
        low = lax.ppermute(
            lax.slice_in_dim(block, block.shape[dim] - width, None, axis=dim), axis, forward
        )
        high = lax.ppermute(lax.slice_in_dim(block, 0, width, axis=dim), axis, backward)
        block = jnp.concatenate([low, block, high], axis=dim)
    return block


def absorb(carry_state, query_heads, key_rows, value_rows):
    running_max, running_sum, weighted = carry_state
    scores = jnp.einsum(
        "thd,khd->htk", query_heads, key_rows, preferred_element_type=jnp.float32
    ) * HEAD_DIM ** (-0.5)
    new_max = jnp.maximum(running_max, jnp.max(scores, axis=-1))
    shrink = jnp.exp(running_max - new_max)
    raised = jnp.exp(scores - new_max[..., None])
    running_sum = running_sum * shrink + jnp.sum(raised, axis=-1)
    weighted = weighted * shrink[..., None] + jnp.einsum(
        "htk,khd->htd", raised.astype(jnp.bfloat16), value_rows, preferred_element_type=jnp.float32
    )
    return (new_max, running_sum, weighted)


def frame_attention(queries, keys, values):
    frames, rows_here, across, channels = queries.shape
    shape5 = (frames, rows_here, across, HEADS, HEAD_DIM)
    scores = jnp.einsum(
        "fywhd,gywhd->ywhfg",
        queries.reshape(shape5),
        keys.reshape(shape5),
        preferred_element_type=jnp.float32,
    ) * HEAD_DIM ** (-0.5)
    frame_ids = jnp.arange(frames)
    allowed = frame_ids[:, None] >= frame_ids[None, :]
    scores = jnp.where(allowed, scores, -1e30)
    peak = jnp.max(scores, axis=-1, keepdims=True)
    raised = jnp.exp(scores - peak)
    totals = jnp.sum(raised, axis=-1)
    blended = jnp.einsum(
        "ywhfg,gywhd->fywhd",
        raised.astype(jnp.bfloat16),
        values.reshape(shape5),
        preferred_element_type=jnp.float32,
    )
    blended = blended / jnp.moveaxis(totals, 3, 0)[..., None]
    return blended.reshape(frames, rows_here, across, channels).astype(jnp.bfloat16)


def attend_frames(triple):
    return frame_attention(triple[0], triple[1], triple[2])


def on_device(
    residual_in, q_spatial, k_spatial, v_spatial, q_temporal, k_temporal, conv_weight, conv_bias
):
    rows_here = q_spatial.shape[1]
    across = q_spatial.shape[2]
    tokens_here = rows_here * across
    query_heads = q_spatial.reshape(tokens_here, HEADS, HEAD_DIM)
    start_state = (
        jnp.full((HEADS, tokens_here), -1e30, jnp.float32),
        jnp.zeros((HEADS, tokens_here), jnp.float32),
        jnp.zeros((HEADS, tokens_here, HEAD_DIM), jnp.float32),
    )
    carry_state = start_state
    key_rows = lax.all_gather(k_spatial, "row", axis=1, tiled=True).reshape(-1, HEADS, HEAD_DIM)
    value_rows = lax.all_gather(v_spatial, "row", axis=1, tiled=True).reshape(-1, HEADS, HEAD_DIM)
    length = key_rows.shape[0]
    block = math.gcd(length, 512)
    for begin in range(0, length, block):
        carry_state = absorb(
            carry_state,
            query_heads,
            key_rows[begin : begin + block],
            value_rows[begin : begin + block],
        )
    running_max, running_sum, weighted = carry_state
    attended = weighted / running_sum[..., None]
    spatial_out = jnp.transpose(attended, (1, 0, 2)).reshape(q_spatial.shape).astype(jnp.bfloat16)
    hidden = (residual_in.astype(jnp.float32) + spatial_out.astype(jnp.float32)).astype(
        jnp.bfloat16
    )
    temporal = attend_frames(
        (
            lax.all_to_all(q_temporal, "frame", split_axis=2, concat_axis=0, tiled=True),
            lax.all_to_all(k_temporal, "frame", split_axis=2, concat_axis=0, tiled=True),
            lax.all_to_all(hidden, "frame", split_axis=2, concat_axis=0, tiled=True),
        )
    )
    returned = lax.all_to_all(temporal, "frame", split_axis=0, concat_axis=2, tiled=True)
    mixed = (hidden.astype(jnp.float32) + returned.astype(jnp.float32)).astype(jnp.bfloat16)
    extended = padded(mixed, (("row", 1),), 1)
    widened = jnp.pad(extended, ((0, 0), (0, 0), (1, 1), (0, 0))).astype(jnp.float32)
    conv = jnp.zeros(mixed.shape, jnp.float32) + conv_bias
    for first in range(3):
        for second in range(3):
            conv = (
                conv
                + conv_weight[first, second]
                * widened[:, first : first + rows_here, second : second + across]
            )
    block_out = (mixed.astype(jnp.float32) + jax.nn.gelu(conv)).astype(jnp.bfloat16)
    return (spatial_out, block_out)


def solution(mesh):
    placed = (
        P("frame", "row", None, None),
        P("frame", "row", None, None),
        P("frame", "row", None, None),
        P("frame", "row", None, None),
        P("frame", "row", None, None),
        P("frame", "row", None, None),
        P(),
        P(),
    )
    return jax.shard_map(
        on_device,
        mesh=mesh,
        in_specs=placed,
        out_specs=(P("frame", "row", None, None), P("frame", "row", None, None)),
        check_vma=False,
    )
```

profile of v0, /device:TPU:1, one launch (start us, length us, event | category | flops | bytes accessed | tf_op | source)
XLA Modules:
  0.0 86.6 jit_solution(11516909779274011631)
XLA Ops:
  0.6 1.0 %copy.56 = bf16[1,1,64,768]{3,1,0,2:T(2,128)(2,1)S(1)} copy(bf16[1,1,64,768]{3,2,1,0:T(8,128)(2,1)} %param.13) | data formatting | bytes 196608 | tf_op args[5]
  1.7 0.5 broadcast.79
  2.2 1.1 %reduce.28 = bf16[64,768]{1,0:T(8,128)(2,1)S(1)} reduce(bf16[64,1,1,768]{3,2,1,0:T(2,128)(2,1)S(1)} %bitcast.61, bf16[]{:T(256)} %broadcast.79), dimensions={1,2}, to_apply=%bitcast.58.reduce_sub_computation | reduce | bytes 196610
  3.3 0.7 reshape.173
  4.0 4.3 %all-to-all-start.2 = ((bf16[4,2,6144]{2,1,0:T(2,128)(2,1)}), bf16[4,2,6144]{2,1,0:T(2,128)(2,1)S(1)}, u32[]{:S(2)}, u32[]{:S(2)}) async-start(bf16[4,2,6144]{2,1,0:T(2,128)(2,1)} %reshape.173), calls=%async_computation.2 | async-start | bytes 196608 | tf_op jit(solution)/shard_map/all_to_all | solution.py:101
  8.2 16.7 %all_gather.7 = bf16[1,8,64,768]{3,2,0,1:T(8,128)(2,1)S(1)} all-gather(bf16[1,1,64,768]{3,2,0,1:T(8,128)(2,1)} %bitcast.67), channel_id=1, replica_groups=mesh['frame'=4,'row'=8] {'row'}, dimensions={1}, use_global_device_ids=true | all-gather | bytes 884736 | tf_op jit(solution)/shard_map/all_gather | solution.py:82
  25.0 1.1 %copy.27 = bf16[1,8,64,768]{2,1,3,0:T(8,128)(2,1)S(1)} copy(bf16[1,8,64,768]{3,2,0,1:T(8,128)(2,1)S(1)} %all_gather.7) | data formatting | bytes 1572864 | tf_op jit(solution)/shard_map/all_gather | solution.py:82
  26.1 0.0 copy-start.1
  26.1 1.0 %reshape.156 = bf16[512,12,64]{0,2,1:T(8,128)(2,1)S(1)} reshape(bf16[1,8,64,768]{2,1,3,0:T(8,128)(2,1)S(1)} %copy.27) | data formatting | bytes 1572864 | tf_op jit(solution)/shard_map/reshape | solution.py:82
  27.1 0.0 copy-done.1
  27.1 15.7 %all_gather.6 = bf16[1,8,64,768]{3,2,0,1:T(8,128)(2,1)S(1)} all-gather(bf16[1,1,64,768]{3,2,0,1:T(8,128)(2,1)S(1)} %bitcast.68), channel_id=1, replica_groups=mesh['frame'=4,'row'=8] {'row'}, dimensions={1}, use_global_device_ids=true | all-gather | bytes 884736 | tf_op jit(solution)/shard_map/all_gather | solution.py:81
  42.8 1.1 %copy.24 = bf16[1,8,64,768]{2,1,3,0:T(8,128)(2,1)S(1)} copy(bf16[1,8,64,768]{3,2,0,1:T(8,128)(2,1)S(1)} %all_gather.6) | data formatting | bytes 1572864 | tf_op jit(solution)/shard_map/all_gather | solution.py:81
  43.9 0.0 copy-start.2
  44.0 1.0 %reshape.155 = bf16[512,12,64]{0,2,1:T(8,128)(2,1)S(1)} reshape(bf16[1,8,64,768]{2,1,3,0:T(8,128)(2,1)S(1)} %copy.24) | data formatting | bytes 1572864 | tf_op jit(solution)/shard_map/reshape | solution.py:81
  44.9 0.0 copy-done.2
  44.9 0.2 reshape.154
  45.1 0.4 fusion.44
  45.6 0.6 fusion
  46.1 0.0 copy-start.3
  46.2 0.5 fusion.5
  46.7 0.0 copy-start.4
  46.7 0.1 copy.28
  46.9 0.2 convert_element_type.89
  47.0 0.0 copy-done.3
  47.0 0.0 copy-start
  47.1 0.2 copy.57
  47.2 1.1 %reduce.29 = bf16[64,768]{1,0:T(8,128)(2,1)S(1)} reduce(bf16[64,1,1,768]{3,2,1,0:T(2,128)(2,1)S(1)} %bitcast.63, bf16[]{:T(256)} %broadcast.79), dimensions={1,2}, to_apply=%bitcast.59.reduce_sub_computation | reduce | bytes 196610
  48.3 0.6 reshape.175
  49.0 0.0 copy-done.4
  49.0 0.2 copy.58
  49.2 1.1 %reduce.30 = bf16[64,768]{1,0:T(8,128)(2,1)S(1)} reduce(bf16[64,1,1,768]{3,2,1,0:T(2,128)(2,1)S(1)} %bitcast.62, bf16[]{:T(256)} %broadcast.79), dimensions={1,2}, to_apply=%bitcast.60.reduce_sub_computation | reduce | bytes 196610
  50.3 0.7 reshape.177
  51.0 0.0 all-to-all-done.2
  51.0 3.9 %all-to-all-start.1 = ((bf16[4,2,6144]{2,1,0:T(2,128)(2,1)}), bf16[4,2,6144]{2,1,0:T(2,128)(2,1)S(1)}, u32[]{:S(2)}, u32[]{:S(2)}) async-start(bf16[4,2,6144]{2,1,0:T(2,128)(2,1)} %reshape.175), calls=%async_computation.1 | async-start | bytes 196608 | tf_op jit(solution)/shard_map/all_to_all | solution.py:100
  54.9 0.1 reshape.174
  55.0 0.5 bitcast_reduce_fusion.2
  55.5 0.2 reshape.159
  55.7 3.0 %all-to-all-done.1 = bf16[4,2,6144]{2,1,0:T(2,128)(2,1)S(1)} async-done(((bf16[4,2,6144]{2,1,0:T(2,128)(2,1)}), bf16[4,2,6144]{2,1,0:T(2,128)(2,1)S(1)}, u32[]{:S(2)}, u32[]{:S(2)}) %all-to-all-start.1) | async-done | bytes 98336 | tf_op jit(solution)/shard_map/all_to_all | solution.py:100
  58.7 0.0 copy-done
  58.7 3.3 %all-to-all-start = ((bf16[4,2,6144]{2,1,0:T(2,128)(2,1)}), bf16[4,2,6144]{2,1,0:T(2,128)(2,1)S(1)}, u32[]{:S(2)}, u32[]{:S(2)}) async-start(bf16[4,2,6144]{2,1,0:T(2,128)(2,1)} %reshape.177), calls=%async_computation | async-start | bytes 196608 | tf_op jit(solution)/shard_map/all_to_all | solution.py:102
  62.0 0.1 reshape.176
  62.1 0.5 bitcast_reduce_fusion.1
  62.6 0.2 reshape.158
  62.8 2.9 %all-to-all-done = bf16[4,2,6144]{2,1,0:T(2,128)(2,1)S(1)} async-done(((bf16[4,2,6144]{2,1,0:T(2,128)(2,1)}), bf16[4,2,6144]{2,1,0:T(2,128)(2,1)S(1)}, u32[]{:S(2)}, u32[]{:S(2)}) %all-to-all-start) | async-done | bytes 98336 | tf_op jit(solution)/shard_map/all_to_all | solution.py:102
  65.7 0.1 reshape.178
  65.8 0.5 bitcast_reduce_fusion
  66.4 0.2 reshape.157
  66.6 0.5 fusion.45
  67.1 0.3 fusion.17
  67.4 0.0 copy-start.5
  67.5 0.5 fusion.7
  68.0 0.0 copy-start.6
  68.0 0.2 convert_element_type.96
  68.2 6.2 %all_to_all.16 = bf16[4,1,16,768]{3,2,1,0:T(8,128)(2,1)S(1)} all-to-all(bf16[4,1,16,768]{3,2,1,0:T(8,128)(2,1)S(1)} %bitcast.65), channel_id=1, replica_groups=mesh['frame'=4,'row'=8] {'frame'}, dimensions={0} | all-to-all | bytes 196608 | tf_op jit(solution)/shard_map/all_to_all | solution.py:105
  74.4 5.8 %collective-permute-start.1 = (bf16[1,1,64,768]{3,2,1,0:T(8,128)(2,1)S(1)}, bf16[1,1,64,768]{3,2,1,0:T(8,128)(2,1)S(1)}, u32[]{:S(2)}, u32[]{:S(2)}) collective-permute-start(bf16[1,1,64,768]{3,2,1,0:T(8,128)(2,1)S(1)} %fusion.38), channel_id=1, source_target_pairs={{1,0},{2,1},{3,2},{4,3},{5,4},{6,5},{7,6},{9,8},{10,9},{11,10},{12... | collective-permute-start | bytes 294920 | tf_op jit(solution)/shard_map/ppermute | solution.py:19
  80.2 3.8 %collective-permute-start = (bf16[1,1,64,768]{3,2,1,0:T(8,128)(2,1)S(1)}, bf16[1,1,64,768]{3,2,1,0:T(8,128)(2,1)S(1)}, u32[]{:S(2)}, u32[]{:S(2)}) collective-permute-start(bf16[1,1,64,768]{3,2,1,0:T(8,128)(2,1)S(1)} %fusion.38), channel_id=1, source_target_pairs={{0,1},{1,2},{2,3},{3,4},{4,5},{5,6},{6,7},{8,9},{9,10},{10,11},{11... | collective-permute-start | bytes 294920 | tf_op jit(solution)/shard_map/ppermute | solution.py:16
  84.0 0.0 copy-done.5
  84.0 0.1 slice_reduce_fusion.8
  84.1 0.3 collective-permute-done.1
  84.3 1.3 %collective-permute-done = bf16[1,1,64,768]{3,2,1,0:T(8,128)(2,1)S(1)} collective-permute-done((bf16[1,1,64,768]{3,2,1,0:T(8,128)(2,1)S(1)}, bf16[1,1,64,768]{3,2,1,0:T(8,128)(2,1)S(1)}, u32[]{:S(2)}, u32[]{:S(2)}) %collective-permute-start) | collective-permute-done | bytes 98336 | tf_op jit(solution)/shard_map/ppermute | solution.py:16
  85.6 0.1 fusion.16
  85.7 0.0 copy-done.6
  85.7 0.9 %fusion.27 = bf16[1,1,64,768]{3,2,1,0:T(8,128)(2,1)} fusion(f32[1,3,66,768]{3,2,1,0:T(8,128)S(1)} %fusion.16, bf16[1,1,64,768]{3,2,1,0:T(8,128)(2,1)S(1)} %fusion.38, f32[768]{0:T(1024)S(1)} %get-tuple-element.9, f32[768]{0:T(1024)S(1)} %get-tuple-element.10, f32[768]{0:T(1024)S(1)} %get-tuple-element.3, f32[768]{0:T(1024)S(1)} %get-tuple-element.4, ...), kind=kLoop, calls=%fused_computation.35 | loop fusion | flops 1425408 | bytes 1996800 | tf_op jit(solution)/shard_map/convert_element_type | solution.py:117
  (6 shorter events, 0.1 us)
Async XLA Ops:
  4.0 47.0 %all-to-all-start.2 = ((bf16[4,2,6144]{2,1,0:T(2,128)(2,1)}), bf16[4,2,6144]{2,1,0:T(2,128)(2,1)S(1)}, u32[]{:S(2)}, u32[]{:S(2)}) async-start(bf16[4,2,6144]{2,1,0:T(2,128)(2,1)} %reshape.173), calls=%async_computation.2 | async-start | bytes 196608 | tf_op jit(solution)/shard_map/all_to_all | solution.py:101
  26.1 1.0 %copy-start.1 = (bf16[1,1,64,768]{3,2,1,0:T(8,128)(2,1)S(1)}, bf16[1,1,64,768]{3,2,1,0:T(8,128)(2,1)}, u32[]{:S(2)}) copy-start(bf16[1,1,64,768]{3,2,1,0:T(8,128)(2,1)} %param.10) | copy-start | bytes 294916
  43.9 1.0 %copy-start.2 = (bf16[1,1,64,768]{3,2,1,0:T(8,128)(2,1)S(1)}, bf16[1,1,64,768]{3,2,1,0:T(8,128)(2,1)}, u32[]{:S(2)}) copy-start(bf16[1,1,64,768]{3,2,1,0:T(8,128)(2,1)} %param.9) | copy-start | bytes 294916
  46.1 0.9 %copy-start.3 = (bf16[1,1,64,768]{3,2,1,0:T(8,128)(2,1)S(1)}, bf16[1,1,64,768]{3,2,1,0:T(8,128)(2,1)}, u32[]{:S(2)}) copy-start(bf16[1,1,64,768]{3,2,1,0:T(8,128)(2,1)} %param.12) | copy-start | bytes 294916
  46.7 2.3 %copy-start.4 = (bf16[1,1,64,768]{3,2,1,0:T(8,128)(2,1)S(1)}, bf16[1,1,64,768]{3,2,1,0:T(8,128)(2,1)}, u32[]{:S(2)}) copy-start(bf16[1,1,64,768]{3,2,1,0:T(8,128)(2,1)} %param.8) | copy-start | bytes 294916
  47.0 11.6 %copy-start = (bf16[1,1,64,768]{3,2,1,0:T(8,128)(2,1)}, bf16[1,1,64,768]{3,2,1,0:T(8,128)(2,1)S(1)}, u32[]{:S(2)}) copy-start(bf16[1,1,64,768]{3,2,1,0:T(8,128)(2,1)S(1)} %convert_element_type.89) | copy-start | bytes 294916
  51.0 7.7 %all-to-all-start.1 = ((bf16[4,2,6144]{2,1,0:T(2,128)(2,1)}), bf16[4,2,6144]{2,1,0:T(2,128)(2,1)S(1)}, u32[]{:S(2)}, u32[]{:S(2)}) async-start(bf16[4,2,6144]{2,1,0:T(2,128)(2,1)} %reshape.175), calls=%async_computation.1 | async-start | bytes 196608 | tf_op jit(solution)/shard_map/all_to_all | solution.py:100
  58.7 7.1 %all-to-all-start = ((bf16[4,2,6144]{2,1,0:T(2,128)(2,1)}), bf16[4,2,6144]{2,1,0:T(2,128)(2,1)S(1)}, u32[]{:S(2)}, u32[]{:S(2)}) async-start(bf16[4,2,6144]{2,1,0:T(2,128)(2,1)} %reshape.177), calls=%async_computation | async-start | bytes 196608 | tf_op jit(solution)/shard_map/all_to_all | solution.py:102
  67.4 16.5 %copy-start.5 = (f32[3,3,768]{2,1,0:T(4,128)S(1)}, f32[3,3,768]{2,1,0:T(4,128)}, u32[]{:S(2)}) copy-start(f32[3,3,768]{2,1,0:T(4,128)} %param.14) | copy-start | bytes 82948
  68.0 17.7 %copy-start.6 = (f32[768]{0:T(1024)S(1)}, f32[768]{0:T(1024)}, u32[]{:S(2)}) copy-start(f32[768]{0:T(1024)} %param.15) | copy-start | bytes 9220
  74.4 9.9 %collective-permute-start.1 = (bf16[1,1,64,768]{3,2,1,0:T(8,128)(2,1)S(1)}, bf16[1,1,64,768]{3,2,1,0:T(8,128)(2,1)S(1)}, u32[]{:S(2)}, u32[]{:S(2)}) collective-permute-start(bf16[1,1,64,768]{3,2,1,0:T(8,128)(2,1)S(1)} %fusion.38), channel_id=1, source_target_pairs={{1,0},{2,1},{3,2},{4,3},{5,4},{6,5},{7,6},{9,8},{10,9},{11,10},{12... | collective-permute-start | bytes 294920 | tf_op jit(solution)/shard_map/ppermute | solution.py:19
  80.2 5.4 %collective-permute-start = (bf16[1,1,64,768]{3,2,1,0:T(8,128)(2,1)S(1)}, bf16[1,1,64,768]{3,2,1,0:T(8,128)(2,1)S(1)}, u32[]{:S(2)}, u32[]{:S(2)}) collective-permute-start(bf16[1,1,64,768]{3,2,1,0:T(8,128)(2,1)S(1)} %fusion.38), channel_id=1, source_target_pairs={{0,1},{1,2},{2,3},{3,4},{4,5},{5,6},{6,7},{8,9},{9,10},{10,11},{11... | collective-permute-start | bytes 294920 | tf_op jit(solution)/shard_map/ppermute | solution.py:16
where the time goes:
time: 87.2 us; the launch traced here: 86.6 us
  blocking collectives  38.6 us (44%)
  starting transfers between devices  21 us (24%)
  local copies, waits for them, and re-layouts  11.2 us (13%)
  waiting for transfers between devices  7.45 us (9%)
  other arithmetic  5.33 us (6%)
  matrix products  2.02 us (2%)
  between operations  0.96 us (1%)
    all_gather x1, blocking collectives, on_device(): lax.all_gather(v_spatial, 'row', axis=1, tiled=True)  16.7 us
    all_gather x1, blocking collectives, on_device(): lax.all_gather(k_spatial, 'row', axis=1, tiled=True)  15.7 us
    all_to_all x1, blocking collectives, on_device(): lax.all_to_all(temporal, 'frame', split_axis=0, concat_axis=2, tiled=True)  6.16 us
    ppermute x1, starting transfers between devices, padded(): lax.ppermute(lax.slice_in_dim(block, 0, width, axis=dim), axis, backward)  5.79 us
    all_to_all x1, starting transfers between devices, on_device(): lax.all_to_all(k_temporal, 'frame', split_axis=2, concat_axis=0, tiled=True)  4.25 us
    unnamed x23, local copies, waits for them, and re-layouts  4.01 us
    all_to_all x1, starting transfers between devices, on_device(): lax.all_to_all(q_temporal, 'frame', split_axis=2, concat_axis=0, tiled=True)  3.9 us
    ppermute x1, starting transfers between devices, padded(): lax.ppermute(lax.slice_in_dim(block, block.shape[dim] - width, None, axis...  3.78 us
  transfers between devices with their start and end apart: 5, of which 4 were waited for; matrix products, arithmetic and copies ran while one was open for 14% of the time, Pallas kernels for 0%

commit v1 on v0

--- a/solution.py
+++ b/solution.py
@@ -3,9 +3,15 @@
 import jax.numpy as jnp
 from jax import lax
 from jax.sharding import PartitionSpec as P
+from jax.lax import all_to_all, axis_size
 
 HEADS = 12
 HEAD_DIM = 64
+
+
+def _play_shards(load, axis_id):
+    r1 = all_to_all(jnp.stack(jnp.split(load, axis_size(axis_id), 2), 0), axis_id, 0, 0)
+    return jnp.concatenate(r1, 0)
 
 
 def padded(block, sides, width):
@@ -97,7 +103,7 @@
     )
     temporal = attend_frames(
         (
-            lax.all_to_all(q_temporal, "frame", split_axis=2, concat_axis=0, tiled=True),
+            _play_shards(q_temporal, "frame"),
             lax.all_to_all(k_temporal, "frame", split_axis=2, concat_axis=0, tiled=True),
             lax.all_to_all(hidden, "frame", split_axis=2, concat_axis=0, tiled=True),
         )

time: 87.2 us -> 85.7 us (0.983)
  local copies, waits for them, and re-layouts: 11.2 us -> 9.89 us
    unnamed x3 -> x2, other arithmetic: 3.35 us -> 2.49 us
    unnamed x23 -> x20, local copies, waits for them, and re-layouts: 4.01 us -> 3.23 us
  transfers between devices with their start and end apart: 5 -> 5, of which waited for: 4 -> 4; matrix products, arithmetic and copies ran while one was open for 14% -> 12% of each run, Pallas kernels for 0% -> 0%
where the time goes in v1:
time: 85.7 us; the launch traced here: 85.1 us
  blocking collectives  38.6 us (45%)
  starting transfers between devices  21 us (25%)
  local copies, waits for them, and re-layouts  9.89 us (12%)
  waiting for transfers between devices  7.45 us (9%)
  other arithmetic  5.11 us (6%)
  matrix products  2.01 us (2%)
  between operations  0.95 us (1%)
    all_gather x1, blocking collectives, on_device(): lax.all_gather(v_spatial, 'row', axis=1, tiled=True)  16.7 us
    all_gather x1, blocking collectives, on_device(): lax.all_gather(k_spatial, 'row', axis=1, tiled=True)  15.7 us
    all_to_all x1, blocking collectives, on_device(): lax.all_to_all(temporal, 'frame', split_axis=0, concat_axis=2, tiled=True)  6.16 us
    ppermute x1, starting transfers between devices, padded(): lax.ppermute(lax.slice_in_dim(block, 0, width, axis=dim), axis, backward)  5.77 us
    all_to_all x1, starting transfers between devices, on_device(): lax.all_to_all(k_temporal, 'frame', split_axis=2, concat_axis=0, tiled=True)  4.25 us
    all_to_all x1, starting transfers between devices, on_device(): lax.all_to_all(hidden, 'frame', split_axis=2, concat_axis=0, tiled=True)  3.91 us
    ppermute x1, starting transfers between devices, padded(): lax.ppermute(lax.slice_in_dim(block, block.shape[dim] - width, None, axis...  3.78 us
    all_to_all x1, starting transfers between devices, _play_shards(): all_to_all(jnp.stack(jnp.split(load, axis_size(axis_id), 2), 0), axis_id,...  3.3 us
  transfers between devices with their start and end apart: 5, of which 4 were waited for; matrix products, arithmetic and copies ran while one was open for 12% of the time, Pallas kernels for 0%

profile of v1, /device:TPU:1, one launch (start us, length us, event | category | flops | bytes accessed | tf_op | source)
XLA Modules:
  0.0 85.1 jit_solution(13488533746869792194)
XLA Ops:
  0.6 1.0 %copy.54 = bf16[1,1,64,768]{3,1,0,2:T(2,128)(2,1)S(1)} copy(bf16[1,1,64,768]{3,2,1,0:T(8,128)(2,1)} %param.13) | data formatting | bytes 196608 | tf_op args[5]
  1.7 0.6 broadcast.78
  2.3 1.2 %reduce.26 = bf16[64,768]{1,0:T(8,128)(2,1)S(1)} reduce(bf16[64,1,1,768]{3,2,1,0:T(2,128)(2,1)S(1)} %bitcast.66, bf16[]{:T(256)} %broadcast.78), dimensions={1,2}, to_apply=%bitcast.64.reduce_sub_computation | reduce | bytes 196610
  3.5 0.7 reshape.167
  4.2 4.3 %all-to-all-start.2 = ((bf16[4,2,6144]{2,1,0:T(2,128)(2,1)}), bf16[4,2,6144]{2,1,0:T(2,128)(2,1)S(1)}, u32[]{:S(2)}, u32[]{:S(2)}) async-start(bf16[4,2,6144]{2,1,0:T(2,128)(2,1)} %reshape.167), calls=%async_computation.2 | async-start | bytes 196608 | tf_op jit(solution)/shard_map/all_to_all | solution.py:107
  8.4 16.7 %all_gather.7 = bf16[1,8,64,768]{3,2,0,1:T(8,128)(2,1)S(1)} all-gather(bf16[1,1,64,768]{3,2,0,1:T(8,128)(2,1)} %bitcast.71), channel_id=1, replica_groups=mesh['frame'=4,'row'=8] {'row'}, dimensions={1}, use_global_device_ids=true | all-gather | bytes 884736 | tf_op jit(solution)/shard_map/all_gather | solution.py:88
  25.2 1.1 %copy.27 = bf16[1,8,64,768]{2,1,3,0:T(8,128)(2,1)S(1)} copy(bf16[1,8,64,768]{3,2,0,1:T(8,128)(2,1)S(1)} %all_gather.7) | data formatting | bytes 1572864 | tf_op jit(solution)/shard_map/all_gather | solution.py:88
  26.3 0.0 copy-start.1
  26.3 1.0 %reshape.151 = bf16[512,12,64]{0,2,1:T(8,128)(2,1)S(1)} reshape(bf16[1,8,64,768]{2,1,3,0:T(8,128)(2,1)S(1)} %copy.27) | data formatting | bytes 1572864 | tf_op jit(solution)/shard_map/reshape | solution.py:88
  27.3 0.0 copy-done.1
  27.3 15.7 %all_gather.6 = bf16[1,8,64,768]{3,2,0,1:T(8,128)(2,1)S(1)} all-gather(bf16[1,1,64,768]{3,2,0,1:T(8,128)(2,1)S(1)} %bitcast.72), channel_id=1, replica_groups=mesh['frame'=4,'row'=8] {'row'}, dimensions={1}, use_global_device_ids=true | all-gather | bytes 884736 | tf_op jit(solution)/shard_map/all_gather | solution.py:87
  43.0 1.1 %copy.24 = bf16[1,8,64,768]{2,1,3,0:T(8,128)(2,1)S(1)} copy(bf16[1,8,64,768]{3,2,0,1:T(8,128)(2,1)S(1)} %all_gather.6) | data formatting | bytes 1572864 | tf_op jit(solution)/shard_map/all_gather | solution.py:87
  44.2 0.0 copy-start.3
  44.2 1.0 %reshape.150 = bf16[512,12,64]{0,2,1:T(8,128)(2,1)S(1)} reshape(bf16[1,8,64,768]{2,1,3,0:T(8,128)(2,1)S(1)} %copy.24) | data formatting | bytes 1572864 | tf_op jit(solution)/shard_map/reshape | solution.py:87
  45.1 0.0 copy-done.3
  45.2 0.2 reshape.149
  45.3 0.4 fusion.44
  45.8 0.6 fusion
  46.4 0.0 copy-start.2
  46.4 0.0 copy-start.4
  46.4 0.5 fusion.5
  46.9 0.1 copy.28
  47.1 0.2 convert_element_type.89
  47.2 0.0 copy-done.2
  47.3 0.0 copy-start
  47.3 0.0 copy-done.4
  47.3 0.2 copy.55
  47.5 1.2 %reduce.27 = bf16[64,768]{1,0:T(8,128)(2,1)S(1)} reduce(bf16[64,1,1,768]{3,2,1,0:T(2,128)(2,1)S(1)} %bitcast.67, bf16[]{:T(256)} %broadcast.78), dimensions={1,2}, to_apply=%bitcast.65.reduce_sub_computation | reduce | bytes 196610
  48.8 0.7 reshape.169
  49.4 0.6 pad_maximum_fusion
  50.1 0.0 all-to-all-done.2
  50.1 3.9 %all-to-all-start = ((bf16[4,2,6144]{2,1,0:T(2,128)(2,1)}), bf16[4,2,6144]{2,1,0:T(2,128)(2,1)S(1)}, u32[]{:S(2)}, u32[]{:S(2)}) async-start(bf16[4,2,6144]{2,1,0:T(2,128)(2,1)} %reshape.169), calls=%async_computation | async-start | bytes 196608 | tf_op jit(solution)/shard_map/all_to_all | solution.py:108
  54.0 0.1 reshape.168
  54.1 0.5 bitcast_reduce_fusion.1
  54.6 0.2 reshape.154
  54.8 3.0 %all-to-all-done = bf16[4,2,6144]{2,1,0:T(2,128)(2,1)S(1)} async-done(((bf16[4,2,6144]{2,1,0:T(2,128)(2,1)}), bf16[4,2,6144]{2,1,0:T(2,128)(2,1)S(1)}, u32[]{:S(2)}, u32[]{:S(2)}) %all-to-all-start) | async-done | bytes 98336 | tf_op jit(solution)/shard_map/all_to_all | solution.py:108
  57.8 3.3 %all-to-all-start.1 = ((bf16[4,1,1,16,768]{4,3,2,1,0:T(8,128)(2,1)}), bf16[4,1,1,16,768]{4,3,2,1,0:T(8,128)(2,1)S(1)}, u32[]{:S(2)}, u32[]{:S(2)}) async-start(bf16[4,1,1,16,768]{4,3,2,1,0:T(8,128)(2,1)} %pad_maximum_fusion), calls=%async_computation.1 | async-start | bytes 196608 | tf_op jit(solution)/shard_map/all_to_all | solution.py:13
  61.1 0.1 reshape.170
  61.2 0.5 bitcast_reduce_fusion
  61.7 0.0 copy-done
  61.7 0.2 reshape.152
  61.9 2.9 %all-to-all-done.1 = bf16[4,1,1,16,768]{4,3,2,1,0:T(8,128)(2,1)S(1)} async-done(((bf16[4,1,1,16,768]{4,3,2,1,0:T(8,128)(2,1)}), bf16[4,1,1,16,768]{4,3,2,1,0:T(8,128)(2,1)S(1)}, u32[]{:S(2)}, u32[]{:S(2)}) %all-to-all-start.1) | async-done | bytes 98336 | tf_op jit(solution)/shard_map/all_to_all | solution.py:13
  64.8 0.2 reshape.153
  65.0 0.5 fusion.45
  65.5 0.3 fusion.17
  65.9 0.0 copy-start.5
  65.9 0.5 fusion.7
  66.4 0.0 copy-start.6
  66.5 0.2 convert_element_type.96
  66.7 6.2 %all_to_all.32 = bf16[4,1,16,768]{3,2,1,0:T(8,128)(2,1)S(1)} all-to-all(bf16[4,1,16,768]{3,2,1,0:T(8,128)(2,1)S(1)} %bitcast.69), channel_id=1, replica_groups=mesh['frame'=4,'row'=8] {'frame'}, dimensions={0} | all-to-all | bytes 196608 | tf_op jit(solution)/shard_map/all_to_all | solution.py:111
  72.9 5.8 %collective-permute-start.1 = (bf16[1,1,64,768]{3,2,1,0:T(8,128)(2,1)S(1)}, bf16[1,1,64,768]{3,2,1,0:T(8,128)(2,1)S(1)}, u32[]{:S(2)}, u32[]{:S(2)}) collective-permute-start(bf16[1,1,64,768]{3,2,1,0:T(8,128)(2,1)S(1)} %fusion.38), channel_id=1, source_target_pairs={{1,0},{2,1},{3,2},{4,3},{5,4},{6,5},{7,6},{9,8},{10,9},{11,10},{12... | collective-permute-start | bytes 294920 | tf_op jit(solution)/shard_map/ppermute | solution.py:25
  78.6 3.8 %collective-permute-start = (bf16[1,1,64,768]{3,2,1,0:T(8,128)(2,1)S(1)}, bf16[1,1,64,768]{3,2,1,0:T(8,128)(2,1)S(1)}, u32[]{:S(2)}, u32[]{:S(2)}) collective-permute-start(bf16[1,1,64,768]{3,2,1,0:T(8,128)(2,1)S(1)} %fusion.38), channel_id=1, source_target_pairs={{0,1},{1,2},{2,3},{3,4},{4,5},{5,6},{6,7},{8,9},{9,10},{10,11},{11... | collective-permute-start | bytes 294920 | tf_op jit(solution)/shard_map/ppermute | solution.py:22
  82.4 0.0 copy-done.5
  82.4 0.1 slice_reduce_fusion.8
  82.5 0.3 collective-permute-done.1
  82.8 1.3 %collective-permute-done = bf16[1,1,64,768]{3,2,1,0:T(8,128)(2,1)S(1)} collective-permute-done((bf16[1,1,64,768]{3,2,1,0:T(8,128)(2,1)S(1)}, bf16[1,1,64,768]{3,2,1,0:T(8,128)(2,1)S(1)}, u32[]{:S(2)}, u32[]{:S(2)}) %collective-permute-start) | collective-permute-done | bytes 98336 | tf_op jit(solution)/shard_map/ppermute | solution.py:22
  84.0 0.1 fusion.16
  84.1 0.0 copy-done.6
  84.1 0.9 %fusion.27 = bf16[1,1,64,768]{3,2,1,0:T(8,128)(2,1)} fusion(f32[1,3,66,768]{3,2,1,0:T(8,128)S(1)} %fusion.16, bf16[1,1,64,768]{3,2,1,0:T(8,128)(2,1)S(1)} %fusion.38, f32[768]{0:T(1024)S(1)} %get-tuple-element.9, f32[768]{0:T(1024)S(1)} %get-tuple-element.10, f32[768]{0:T(1024)S(1)} %get-tuple-element.3, f32[768]{0:T(1024)S(1)} %get-tuple-element.4, ...), kind=kLoop, calls=%fused_computation.35 | loop fusion | flops 1425408 | bytes 1996800 | tf_op jit(solution)/shard_map/convert_element_type | solution.py:123
  (7 shorter events, 0.1 us)
Async XLA Ops:
  4.2 45.9 %all-to-all-start.2 = ((bf16[4,2,6144]{2,1,0:T(2,128)(2,1)}), bf16[4,2,6144]{2,1,0:T(2,128)(2,1)S(1)}, u32[]{:S(2)}, u32[]{:S(2)}) async-start(bf16[4,2,6144]{2,1,0:T(2,128)(2,1)} %reshape.167), calls=%async_computation.2 | async-start | bytes 196608 | tf_op jit(solution)/shard_map/all_to_all | solution.py:107
  26.3 1.0 %copy-start.1 = (bf16[1,1,64,768]{3,2,1,0:T(8,128)(2,1)S(1)}, bf16[1,1,64,768]{3,2,1,0:T(8,128)(2,1)}, u32[]{:S(2)}) copy-start(bf16[1,1,64,768]{3,2,1,0:T(8,128)(2,1)} %param.10) | copy-start | bytes 294916
  44.2 1.0 %copy-start.3 = (bf16[1,1,64,768]{3,2,1,0:T(8,128)(2,1)S(1)}, bf16[1,1,64,768]{3,2,1,0:T(8,128)(2,1)}, u32[]{:S(2)}) copy-start(bf16[1,1,64,768]{3,2,1,0:T(8,128)(2,1)} %param.9) | copy-start | bytes 294916
  46.4 0.9 %copy-start.2 = (bf16[1,1,64,768]{3,2,1,0:T(8,128)(2,1)S(1)}, bf16[1,1,64,768]{3,2,1,0:T(8,128)(2,1)}, u32[]{:S(2)}) copy-start(bf16[1,1,64,768]{3,2,1,0:T(8,128)(2,1)} %param.12) | copy-start | bytes 294916
  46.4 0.9 %copy-start.4 = (bf16[1,1,64,768]{3,2,1,0:T(8,128)(2,1)S(1)}, bf16[1,1,64,768]{3,2,1,0:T(8,128)(2,1)}, u32[]{:S(2)}) copy-start(bf16[1,1,64,768]{3,2,1,0:T(8,128)(2,1)} %param.8) | copy-start | bytes 294916
  47.3 14.5 %copy-start = (bf16[1,1,64,768]{3,2,1,0:T(8,128)(2,1)}, bf16[1,1,64,768]{3,2,1,0:T(8,128)(2,1)S(1)}, u32[]{:S(2)}) copy-start(bf16[1,1,64,768]{3,2,1,0:T(8,128)(2,1)S(1)} %convert_element_type.89) | copy-start | bytes 294916
  50.1 7.7 %all-to-all-start = ((bf16[4,2,6144]{2,1,0:T(2,128)(2,1)}), bf16[4,2,6144]{2,1,0:T(2,128)(2,1)S(1)}, u32[]{:S(2)}, u32[]{:S(2)}) async-start(bf16[4,2,6144]{2,1,0:T(2,128)(2,1)} %reshape.169), calls=%async_computation | async-start | bytes 196608 | tf_op jit(solution)/shard_map/all_to_all | solution.py:108
  57.8 7.1 %all-to-all-start.1 = ((bf16[4,1,1,16,768]{4,3,2,1,0:T(8,128)(2,1)}), bf16[4,1,1,16,768]{4,3,2,1,0:T(8,128)(2,1)S(1)}, u32[]{:S(2)}, u32[]{:S(2)}) async-start(bf16[4,1,1,16,768]{4,3,2,1,0:T(8,128)(2,1)} %pad_maximum_fusion), calls=%async_computation.1 | async-start | bytes 196608 | tf_op jit(solution)/shard_map/all_to_all | solution.py:13
  65.9 16.5 %copy-start.5 = (f32[3,3,768]{2,1,0:T(4,128)S(1)}, f32[3,3,768]{2,1,0:T(4,128)}, u32[]{:S(2)}) copy-start(f32[3,3,768]{2,1,0:T(4,128)} %param.14) | copy-start | bytes 82948
  66.4 17.7 %copy-start.6 = (f32[768]{0:T(1024)S(1)}, f32[768]{0:T(1024)}, u32[]{:S(2)}) copy-start(f32[768]{0:T(1024)} %param.15) | copy-start | bytes 9220
  72.9 9.9 %collective-permute-start.1 = (bf16[1,1,64,768]{3,2,1,0:T(8,128)(2,1)S(1)}, bf16[1,1,64,768]{3,2,1,0:T(8,128)(2,1)S(1)}, u32[]{:S(2)}, u32[]{:S(2)}) collective-permute-start(bf16[1,1,64,768]{3,2,1,0:T(8,128)(2,1)S(1)} %fusion.38), channel_id=1, source_target_pairs={{1,0},{2,1},{3,2},{4,3},{5,4},{6,5},{7,6},{9,8},{10,9},{11,10},{12... | collective-permute-start | bytes 294920 | tf_op jit(solution)/shard_map/ppermute | solution.py:25
  78.6 5.4 %collective-permute-start = (bf16[1,1,64,768]{3,2,1,0:T(8,128)(2,1)S(1)}, bf16[1,1,64,768]{3,2,1,0:T(8,128)(2,1)S(1)}, u32[]{:S(2)}, u32[]{:S(2)}) collective-permute-start(bf16[1,1,64,768]{3,2,1,0:T(8,128)(2,1)S(1)} %fusion.38), channel_id=1, source_target_pairs={{0,1},{1,2},{2,3},{3,4},{4,5},{5,6},{6,7},{8,9},{9,10},{10,11},{11... | collective-permute-start | bytes 294920 | tf_op jit(solution)/shard_map/ppermute | solution.py:22
